TPU v7x, 256 devices: a whole 4x4x8 slice. The times are simulated.
256 devices in a mesh: train: 16 (over z, core), query: 16 (over y, x).
Axes of the slice: x: 4, y: 4, z: 8, core: 2. Of those that a mesh axis runs over, the one named last changes fastest.
Arguments:
- train_hidden: bfloat16 [512, 96, 4096], P(('train', 'query')), may hold values from -6 to 6
- train_outgrad: bfloat16 [512, 96, 14336], P(('train', 'query')), may hold values from -6 to 6
- train_mask: int32 [512, 96], P(('train', 'query')), may hold values 0 or 1
- query_hidden: bfloat16 [256, 96, 4096], P(('train', 'query')), may hold values from -6 to 6
- query_outgrad: bfloat16 [256, 96, 14336], P(('train', 'query')), may hold values from -6 to 6
- query_mask: int32 [256, 96], P(('train', 'query')), may hold values 0 or 1
- proj_in: bfloat16 [4096, 64], replicated, may hold values from -0.09375 to 0.09375
- proj_out: bfloat16 [14336, 64], replicated, may hold values from -0.046875 to 0.046875
Outputs:
- scores: float32 [512, 256], P(('train', 'query'))
All inputs are finite; a program needn't handle non-finite values. No bound on the sum of `train_mask` or of `query_mask` on one device may be relied on, other than what follows from the above.
Results may differ from a plain program's by a relative error of at most 0.0003.
Values sent between devices are 32-bit elements; how exact they have to be, the bound alone decides.
A program may use at most 128 MiB of HBM per device.

v0:
```python
import jax
import jax.numpy as jnp
from jax import lax
from jax.sharding import PartitionSpec as P

damping_share = 0.1
AXES = ("train", "query")
HIGHEST = lax.Precision.HIGHEST


def sketch_terms(hidden, outgrad, mask, proj_in, proj_out):
    proof_count, token_count, model_width = hidden.shape
    input_side = jnp.dot(
        hidden.reshape(proof_count * token_count, model_width),
        proj_in,
        preferred_element_type=jnp.float32,
    )
    output_side = jnp.dot(
        outgrad.reshape(proof_count * token_count, -1), proj_out, preferred_element_type=jnp.float32
    )
    output_side = output_side * mask.reshape(-1, 1).astype(jnp.float32)
    input_side = input_side.reshape(proof_count, token_count, -1)
    output_side = output_side.reshape(proof_count, token_count, -1)
    outer_sum = jnp.einsum("pti,ptj->pij", output_side, input_side, precision=HIGHEST)
    return outer_sum.reshape(proof_count, -1)


def spd_solve(system, right, tolerance=1e-3, most_steps=48):
    size = system.shape[0]
    eye = jnp.eye(size, dtype=system.dtype)
    diagonal = jnp.sum(system * eye, axis=1)
    inv_sqrt = lax.rsqrt(diagonal)
    bound = jnp.max(jnp.sum(jnp.abs(system) * inv_sqrt[:, None] * inv_sqrt[None, :], axis=1))
    start = eye * (1.0 / (diagonal * bound))[None, :]

    def going(carry):
        step, _, residual = carry
        return (step < most_steps) & (residual > tolerance)

    def advance(carry):
        step, inverse, _ = carry
        remainder = eye - jnp.dot(system, inverse, precision=HIGHEST)
        residual = jnp.sqrt(jnp.sum(remainder * remainder))
        return step + 1, inverse + jnp.dot(inverse, remainder, precision=HIGHEST), residual

    _, inverse, _ = lax.while_loop(
        going, advance, (jnp.int32(0), start, jnp.array(jnp.inf, system.dtype))
    )
    solved = jnp.dot(inverse, right, precision=HIGHEST)
    return solved + jnp.dot(
        inverse, right - jnp.dot(system, solved, precision=HIGHEST), precision=HIGHEST
    )


def body(
    train_hidden,
    train_outgrad,
    train_mask,
    query_hidden,
    query_outgrad,
    query_mask,
    proj_in,
    proj_out,
):
    train_sketch = sketch_terms(train_hidden, train_outgrad, train_mask, proj_in, proj_out)
    query_sketch = sketch_terms(query_hidden, query_outgrad, query_mask, proj_in, proj_out)
    block_rows = train_sketch.shape[0]
    width = train_sketch.shape[1]
    both = jnp.concatenate([train_sketch, query_sketch], axis=0)
    within = lax.all_gather(both.reshape(1, -1), AXES[1], axis=0, tiled=True)
    everyone = lax.all_gather(within, AXES[0], axis=0, tiled=True)
    devices = everyone.shape[0]
    pieces = [everyone[:, r * width:(r + 1) * width] for r in range(block_rows + 1)]
    gram_matrix = jnp.concatenate(
        [
            jnp.concatenate(
                [jnp.dot(pieces[r], pieces[c].T, precision=HIGHEST) for c in range(block_rows)],
                axis=1,
            )
            for r in range(block_rows)
        ],
        axis=0,
    )
    products = jnp.concatenate(
        [jnp.dot(pieces[r], pieces[block_rows].T, precision=HIGHEST) for r in range(block_rows)],
        axis=0,
    )
    total_rows = gram_matrix.shape[0]
    eye = jnp.eye(total_rows, dtype=jnp.float32)
    damping = damping_share * jnp.sum(gram_matrix * eye) / total_rows
    system = gram_matrix + damping * eye
    solved = total_rows * spd_solve(system, products)
    me = lax.axis_index(AXES)
    return jnp.concatenate(
        [lax.dynamic_slice_in_dim(solved, r * devices + me, 1, 0) for r in range(block_rows)],
        axis=0,
    )


def solution(mesh):
    in_specs = (
        P(AXES, None, None),
        P(AXES, None, None),
        P(AXES, None),
        P(AXES, None, None),
        P(AXES, None, None),
        P(AXES, None),
        P(),
        P(),
    )
    out_specs = P(AXES, None)
    return jax.shard_map(body, mesh=mesh, in_specs=in_specs, out_specs=out_specs, check_vma=False)
```

profile of v0, /device:TPU:1, one launch (start us, length us, event | category | flops | bytes accessed | tf_op | source)
XLA Modules:
  0.0 310.8 jit_solution(11903594564496950040)
XLA Ops:
  6.5 0.8 convert_bitcast_fusion
  7.3 0.7 convert_element_type.26
  8.1 1.6 fusion.26
  9.8 2.4 fusion.22
  12.5 5.1 %convolution_multiply_fusion = f32[192,64]{0,1:T(8,128)S(1)} fusion(bf16[192,14336]{1,0:T(8,128)(2,1)} %bitcast.50, bf16[14336,64]{0,1:T(8,128)(2,1)} %param.17, f32[192]{0:T(256)S(1)} %convert_element_type.27), kind=kOutput, calls=%fused_computation.27 | convolution fusion | flops 352333824 | bytes 7389952 | tf_op jit(solution)/shard_map/dot_general | solution.py:18
  17.7 2.1 fusion.28
  20.2 20.3 %all-gather = f32[16,1,12288]{2,1,0:T(1,128)S(1)} all-gather(f32[1,1,12288]{2,1,0:T(1,128)S(1)} %reshape.68), channel_id=1, replica_groups=mesh['train'=16,'query'=16] {'query'}, dimensions={0}, use_global_device_ids=true | all-gather | bytes 835584 | tf_op jit(solution)/shard_map/all_gather | solution.py:70
  40.5 1.4 copy.17
  41.9 82.2 %all-gather.3.cloned.1.call-done = f32[256,12288]{1,0:T(8,128)} async-done(((f32[16,12288]{1,0:T(8,128)}), f32[256,12288]{1,0:T(8,128)}) %all-gather.3.cloned.1.call-update) | async-done | bytes 12582928 | tf_op jit(solution)/shard_map/all_gather | solution.py:71
  124.2 11.5 %fusion.10 = f32[256,256]{0,1:T(8,128)S(1)} fusion(f32[256,12288]{1,0:T(8,128)} %all-gather.3.cloned.1.call-done), kind=kOutput, calls=%fused_computation.13 | convolution fusion | flops 3221225472 | bytes 8650752 | tf_op jit(solution)/shard_map/dot_general | solution.py:77
  135.7 11.6 %fusion.8 = f32[256,256]{0,1:T(8,128)S(1)} fusion(f32[256,12288]{1,0:T(8,128)} %all-gather.3.cloned.1.call-done), kind=kOutput, calls=%fused_computation.11 | convolution fusion | flops 3221225472 | bytes 4456448 | tf_op jit(solution)/shard_map/dot_general | solution.py:77
  147.3 3.5 %fusion.12 = f32[256,256]{0,1:T(8,128)S(1)} fusion(f32[256,12288]{1,0:T(8,128)S(1)} %copy-done.2), kind=kOutput, calls=%fused_computation.15 | convolution fusion | flops 3221225472 | bytes 8650752 | tf_op jit(solution)/shard_map/dot_general | solution.py:77
  150.8 3.5 %fusion.17 = f32[256,256]{0,1:T(8,128)S(1)} fusion(f32[256,12288]{1,0:T(8,128)S(1)} %copy-done.2), kind=kOutput, calls=%fused_computation.20 | convolution fusion | flops 3221225472 | bytes 4456448 | tf_op jit(solution)/shard_map/dot_general | solution.py:77
  154.4 0.7 copy-done.5
  155.1 0.7 select_reduce_fusion.1
  156.4 2.1 select_reduce_fusion
  158.5 2.5 copy.12
  161.0 1.4 multiply_reduce_fusion.1
  162.4 0.7 reduce_max.9
  163.1 0.6 multiply_divide_fusion
  163.7 1.2 fusion.25
  164.9 109.6 %while.13 = (s32[]{:T(128)}, f32[512,512]{0,1:T(8,128)}, f32[]{:T(128)}, f32[512,512]{1,0:T(8,128)}, s32[]{:T(128)}) while((s32[]{:T(128)}, f32[512,512]{0,1:T(8,128)}, f32[]{:T(128)}, f32[512,512]{1,0:T(8,128)}, s32[]{:T(128)}) %tuple.28), condition=%wide.region_6.0_spmd.clone, body=%wide.region_4.0_spmd.clone.sunk | while | flops 3222798336 | bytes 12583025 | solution.py:46
  164.9 1.2 copy.31
  166.1 1.0 copy-done.1
  167.1 4.7 %multiply_reduce_fusion.3 = (f32[]{:T(128)}, f32[512,512]{1,0:T(8,128)}) fusion(f32[512,512]{1,0:T(8,128)} %get-tuple-element.106, f32[512,512]{0,1:T(8,128)S(1)} %copy.31), kind=kOutput, calls=%fused_computation.5.clone.1 | convolution fusion | flops 1611923456 | bytes 3145732 | tf_op jit(solution)/shard_map/while/body/dot_general | solution.py:42
  172.4 4.7 %fusion.61 = f32[512,512]{0,1:T(8,128)} fusion(f32[512,512]{0,1:T(8,128)} %copy-done.1, f32[512,512]{1,0:T(8,128)} %get-tuple-element.91), kind=kOutput, calls=%fused_computation.2.clone.1 | convolution fusion | flops 1610874880 | bytes 3145728 | tf_op jit(solution)/shard_map/while/body/dot_general | solution.py:44
  177.1 1.2 copy.31
  178.3 1.0 copy-done.1
  179.3 4.7 %multiply_reduce_fusion.3 = (f32[]{:T(128)}, f32[512,512]{1,0:T(8,128)}) fusion(f32[512,512]{1,0:T(8,128)} %get-tuple-element.106, f32[512,512]{0,1:T(8,128)S(1)} %copy.31), kind=kOutput, calls=%fused_computation.5.clone.1 | convolution fusion | flops 1611923456 | bytes 3145732 | tf_op jit(solution)/shard_map/while/body/dot_general | solution.py:42
  184.6 4.7 %fusion.61 = f32[512,512]{0,1:T(8,128)} fusion(f32[512,512]{0,1:T(8,128)} %copy-done.1, f32[512,512]{1,0:T(8,128)} %get-tuple-element.91), kind=kOutput, calls=%fused_computation.2.clone.1 | convolution fusion | flops 1610874880 | bytes 3145728 | tf_op jit(solution)/shard_map/while/body/dot_general | solution.py:44
  189.3 1.2 copy.31
  190.5 1.0 copy-done.1
  191.5 4.7 %multiply_reduce_fusion.3 = (f32[]{:T(128)}, f32[512,512]{1,0:T(8,128)}) fusion(f32[512,512]{1,0:T(8,128)} %get-tuple-element.106, f32[512,512]{0,1:T(8,128)S(1)} %copy.31), kind=kOutput, calls=%fused_computation.5.clone.1 | convolution fusion | flops 1611923456 | bytes 3145732 | tf_op jit(solution)/shard_map/while/body/dot_general | solution.py:42
  196.8 4.7 %fusion.61 = f32[512,512]{0,1:T(8,128)} fusion(f32[512,512]{0,1:T(8,128)} %copy-done.1, f32[512,512]{1,0:T(8,128)} %get-tuple-element.91), kind=kOutput, calls=%fused_computation.2.clone.1 | convolution fusion | flops 1610874880 | bytes 3145728 | tf_op jit(solution)/shard_map/while/body/dot_general | solution.py:44
  201.5 1.2 copy.31
  202.7 1.0 copy-done.1
  203.7 4.7 %multiply_reduce_fusion.3 = (f32[]{:T(128)}, f32[512,512]{1,0:T(8,128)}) fusion(f32[512,512]{1,0:T(8,128)} %get-tuple-element.106, f32[512,512]{0,1:T(8,128)S(1)} %copy.31), kind=kOutput, calls=%fused_computation.5.clone.1 | convolution fusion | flops 1611923456 | bytes 3145732 | tf_op jit(solution)/shard_map/while/body/dot_general | solution.py:42
  209.0 4.7 %fusion.61 = f32[512,512]{0,1:T(8,128)} fusion(f32[512,512]{0,1:T(8,128)} %copy-done.1, f32[512,512]{1,0:T(8,128)} %get-tuple-element.91), kind=kOutput, calls=%fused_computation.2.clone.1 | convolution fusion | flops 1610874880 | bytes 3145728 | tf_op jit(solution)/shard_map/while/body/dot_general | solution.py:44
  213.7 1.2 copy.31
  214.9 1.0 copy-done.1
  215.9 4.7 %multiply_reduce_fusion.3 = (f32[]{:T(128)}, f32[512,512]{1,0:T(8,128)}) fusion(f32[512,512]{1,0:T(8,128)} %get-tuple-element.106, f32[512,512]{0,1:T(8,128)S(1)} %copy.31), kind=kOutput, calls=%fused_computation.5.clone.1 | convolution fusion | flops 1611923456 | bytes 3145732 | tf_op jit(solution)/shard_map/while/body/dot_general | solution.py:42
  221.1 4.7 %fusion.61 = f32[512,512]{0,1:T(8,128)} fusion(f32[512,512]{0,1:T(8,128)} %copy-done.1, f32[512,512]{1,0:T(8,128)} %get-tuple-element.91), kind=kOutput, calls=%fused_computation.2.clone.1 | convolution fusion | flops 1610874880 | bytes 3145728 | tf_op jit(solution)/shard_map/while/body/dot_general | solution.py:44
  225.8 1.2 copy.31
  227.1 1.0 copy-done.1
  228.0 4.7 %multiply_reduce_fusion.3 = (f32[]{:T(128)}, f32[512,512]{1,0:T(8,128)}) fusion(f32[512,512]{1,0:T(8,128)} %get-tuple-element.106, f32[512,512]{0,1:T(8,128)S(1)} %copy.31), kind=kOutput, calls=%fused_computation.5.clone.1 | convolution fusion | flops 1611923456 | bytes 3145732 | tf_op jit(solution)/shard_map/while/body/dot_general | solution.py:42
  233.3 4.7 %fusion.61 = f32[512,512]{0,1:T(8,128)} fusion(f32[512,512]{0,1:T(8,128)} %copy-done.1, f32[512,512]{1,0:T(8,128)} %get-tuple-element.91), kind=kOutput, calls=%fused_computation.2.clone.1 | convolution fusion | flops 1610874880 | bytes 3145728 | tf_op jit(solution)/shard_map/while/body/dot_general | solution.py:44
  238.0 1.2 copy.31
  239.2 1.0 copy-done.1
  240.2 4.7 %multiply_reduce_fusion.3 = (f32[]{:T(128)}, f32[512,512]{1,0:T(8,128)}) fusion(f32[512,512]{1,0:T(8,128)} %get-tuple-element.106, f32[512,512]{0,1:T(8,128)S(1)} %copy.31), kind=kOutput, calls=%fused_computation.5.clone.1 | convolution fusion | flops 1611923456 | bytes 3145732 | tf_op jit(solution)/shard_map/while/body/dot_general | solution.py:42
  245.5 4.7 %fusion.61 = f32[512,512]{0,1:T(8,128)} fusion(f32[512,512]{0,1:T(8,128)} %copy-done.1, f32[512,512]{1,0:T(8,128)} %get-tuple-element.91), kind=kOutput, calls=%fused_computation.2.clone.1 | convolution fusion | flops 1610874880 | bytes 3145728 | tf_op jit(solution)/shard_map/while/body/dot_general | solution.py:44
  250.2 1.2 copy.31
  251.4 1.0 copy-done.1
  252.4 4.7 %multiply_reduce_fusion.3 = (f32[]{:T(128)}, f32[512,512]{1,0:T(8,128)}) fusion(f32[512,512]{1,0:T(8,128)} %get-tuple-element.106, f32[512,512]{0,1:T(8,128)S(1)} %copy.31), kind=kOutput, calls=%fused_computation.5.clone.1 | convolution fusion | flops 1611923456 | bytes 3145732 | tf_op jit(solution)/shard_map/while/body/dot_general | solution.py:42
  257.7 4.7 %fusion.61 = f32[512,512]{0,1:T(8,128)} fusion(f32[512,512]{0,1:T(8,128)} %copy-done.1, f32[512,512]{1,0:T(8,128)} %get-tuple-element.91), kind=kOutput, calls=%fused_computation.2.clone.1 | convolution fusion | flops 1610874880 | bytes 3145728 | tf_op jit(solution)/shard_map/while/body/dot_general | solution.py:44
  262.4 1.2 copy.31
  263.6 1.0 copy-done.1
  264.6 4.7 %multiply_reduce_fusion.3 = (f32[]{:T(128)}, f32[512,512]{1,0:T(8,128)}) fusion(f32[512,512]{1,0:T(8,128)} %get-tuple-element.106, f32[512,512]{0,1:T(8,128)S(1)} %copy.31), kind=kOutput, calls=%fused_computation.5.clone.1 | convolution fusion | flops 1611923456 | bytes 3145732 | tf_op jit(solution)/shard_map/while/body/dot_general | solution.py:42
  269.9 4.7 %fusion.61 = f32[512,512]{0,1:T(8,128)} fusion(f32[512,512]{0,1:T(8,128)} %copy-done.1, f32[512,512]{1,0:T(8,128)} %get-tuple-element.91), kind=kOutput, calls=%fused_computation.2.clone.1 | convolution fusion | flops 1610874880 | bytes 3145728 | tf_op jit(solution)/shard_map/while/body/dot_general | solution.py:44
  274.6 11.4 %fusion.3 = f32[256,256]{1,0:T(8,128)S(1)} fusion(f32[256,12288]{1,0:T(8,128)} %all-gather.3.cloned.1.call-done), kind=kOutput, calls=%fused_computation.6 | convolution fusion | flops 3221225472 | bytes 8650752 | tf_op jit(solution)/shard_map/dot_general | solution.py:85
  286.0 11.8 %fusion.5 = f32[256,256]{1,0:T(8,128)S(1)} fusion(f32[256,12288]{1,0:T(8,128)} %all-gather.3.cloned.1.call-done), kind=kOutput, calls=%fused_computation.8 | convolution fusion | flops 3221225472 | bytes 8650752 | tf_op jit(solution)/shard_map/dot_general | solution.py:85
  297.9 1.8 fusion.30
  299.7 1.8 convolution_subtract_fusion.1
  301.5 1.8 fusion.21
  303.4 0.6 pad_maximum_fusion.3
  (32 shorter events, 1.0 us)
Async XLA Ops:
  6.5 3.2 %copy-start = (bf16[1,96,14336]{2,1,0:T(8,128)(2,1)S(1)}, bf16[1,96,14336]{2,1,0:T(8,128)(2,1)}, u32[]{:S(2)}) copy-start(bf16[1,96,14336]{2,1,0:T(8,128)(2,1)} %param.14) | copy-start | bytes 8257540
  6.5 117.6 %all-gather.3.cloned.1.call-start = ((), (), s32[]{:S(2)}) async-start(), calls=%async_computation | async-start | bytes 13369344 | tf_op jit(solution)/shard_map/all_gather | solution.py:71
  12.5 5.2 %copy-start.6 = (bf16[4096,64]{0,1:T(8,128)(2,1)S(1)}, bf16[4096,64]{0,1:T(8,128)(2,1)}, u32[]{:S(2)}) copy-start(bf16[4096,64]{0,1:T(8,128)(2,1)} %param.16) | copy-start | bytes 1572868
  124.2 23.1 %copy-start.2 = (f32[256,12288]{1,0:T(8,128)S(1)}, f32[256,12288]{1,0:T(8,128)}, u32[]{:S(2)}) copy-start(f32[256,12288]{1,0:T(8,128)} %all-gather.3.cloned.1.call-done) | copy-start | bytes 37748740
  154.4 0.7 copy-start.5
  166.1 1.0 copy-start.1
  178.3 1.0 copy-start.1
  190.5 1.0 copy-start.1
  202.7 1.0 copy-start.1
  214.9 1.0 copy-start.1
  227.1 1.0 copy-start.1
  239.2 1.0 copy-start.1
  251.4 1.0 copy-start.1
  263.6 1.0 copy-start.1
  286.0 11.9 %copy-start.3 = (f32[512,512]{0,1:T(8,128)S(1)}, f32[512,512]{0,1:T(8,128)}, u32[]{:S(2)}) copy-start(f32[512,512]{0,1:T(8,128)} %get-tuple-element.32) | copy-start | bytes 3145732
  286.0 13.7 %copy-start.4 = (f32[512,512]{0,1:T(8,128)S(1)}, f32[512,512]{0,1:T(8,128)}, u32[]{:S(2)}) copy-start(f32[512,512]{0,1:T(8,128)} %get-tuple-element.60) | copy-start | bytes 3145732
Sparse Core Ops, SparseCore 0:
  42.1 82.0 all-gather.2
where the time goes:
time: 312 us; the launch traced here: 311 us
  matrix products  155 us (50%)
  waiting for transfers between devices  82.2 us (26%)
  local copies, waits for them, and re-layouts  24.9 us (8%)
  blocking collectives  20.3 us (7%)
  between operations  14.2 us (5%)
  other arithmetic  8.84 us (3%)
  loops' own time  5.5 us (2%)
    all_gather x1, waiting for transfers between devices, body(): everyone = lax.all_gather(within, AXES[0], axis=0, tiled=True)  82.2 us
    dot_general x9, matrix products, advance(): jnp.dot(inverse, remainder, precision=HIGHEST)  42.3 us
    dot_general x9, matrix products, advance(): remainder = eye - jnp.dot(system, inverse, precision=HIGHEST)  42 us
    dot_general x4, matrix products, body(): jnp.dot(pieces[r], pieces[c].T, precision=HIGHEST)  30.2 us
    dot_general x2, matrix products, body(): jnp.dot(pieces[r], pieces[block_rows].T, precision=HIGHEST)  23.3 us
    all_gather x1, blocking collectives, body(): within = lax.all_gather(both.reshape(1, -1), AXES[1], axis=0, tiled=True)  20.3 us
    while x27, local copies, waits for them, and re-layouts  19.8 us
    dot_general x2, matrix products, sketch_terms(): jnp.dot(outgrad.reshape(proof_count * token_count, -1), proj_out, preferr...  7.41 us
  transfers between devices with their start and end apart: 1, of which 1 were waited for; matrix products, arithmetic and copies ran while one was open for 0% of the time, Pallas kernels for 0%

commit v1 on v0

--- a/solution.py
+++ b/solution.py
@@ -89,6 +89,7 @@
     eye = jnp.eye(total_rows, dtype=jnp.float32)
     damping = damping_share * jnp.sum(gram_matrix * eye) / total_rows
     system = gram_matrix + damping * eye
+    system, products = lax.optimization_barrier((system, products))
     solved = total_rows * spd_solve(system, products)
     me = lax.axis_index(AXES)
     return jnp.concatenate(

time: 312 us -> 290 us (0.929)
  matrix products: 155 us -> 140 us
  local copies, waits for them, and re-layouts: 24.9 us -> 17.4 us
    dot_general x9 -> x10, matrix products: 42.3 us -> 28.9 us  [advance(): jnp.dot(inverse, remainder, precision=HIGHEST)]
    while x27 -> x10, local copies, waits for them, and re-layouts: 19.8 us -> 12.3 us
    dot_general x9 -> x10, matrix products: 42 us -> 38.3 us  [advance(): remainder = eye - jnp.dot(system, inverse, precision=HIGHEST)]
where the time goes in v1:
time: 290 us; the launch traced here: 289 us
  matrix products  140 us (48%)
  waiting for transfers between devices  82.2 us (28%)
  blocking collectives  20.3 us (7%)
  local copies, waits for them, and re-layouts  17.4 us (6%)
  between operations  14.4 us (5%)
  other arithmetic  7.38 us (3%)
  loops' own time  7.07 us (2%)
    all_gather x1, waiting for transfers between devices, body(): everyone = lax.all_gather(within, AXES[0], axis=0, tiled=True)  82.2 us
    dot_general x10, matrix products, advance(): remainder = eye - jnp.dot(system, inverse, precision=HIGHEST)  38.3 us
    dot_general x4, matrix products, body(): jnp.dot(pieces[r], pieces[c].T, precision=HIGHEST)  30.2 us
    dot_general x10, matrix products, advance(): jnp.dot(inverse, remainder, precision=HIGHEST)  28.9 us
    dot_general x2, matrix products, body(): jnp.dot(pieces[r], pieces[block_rows].T, precision=HIGHEST)  23.5 us
    all_gather x1, blocking collectives, body(): within = lax.all_gather(both.reshape(1, -1), AXES[1], axis=0, tiled=True)  20.3 us
    while x10, local copies, waits for them, and re-layouts  12.3 us
    dot_general x2, matrix products, sketch_terms(): jnp.dot(outgrad.reshape(proof_count * token_count, -1), proj_out, preferr...  7.41 us
  transfers between devices with their start and end apart: 1, of which 1 were waited for; matrix products, arithmetic and copies ran while one was open for 0% of the time, Pallas kernels for 0%

profile of v1, /device:TPU:1, one launch (start us, length us, event | category | flops | bytes accessed | tf_op | source)
XLA Modules:
  0.0 288.9 jit_solution(14806697937698070990)
XLA Ops:
  6.5 0.8 convert_element_type.26
  7.4 0.1 convert_element_type.27
  7.5 5.1 %convolution_multiply_fusion = f32[192,64]{0,1:T(8,128)S(1)} fusion(bf16[192,14336]{1,0:T(8,128)(2,1)} %bitcast.51, bf16[14336,64]{0,1:T(8,128)(2,1)} %param.17, f32[192]{0:T(256)S(1)} %convert_element_type.27), kind=kOutput, calls=%fused_computation.27 | convolution fusion | flops 352333824 | bytes 7389952 | tf_op jit(solution)/shard_map/dot_general | solution.py:18
  12.5 0.1 reshape.62
  12.6 2.1 fusion.28
  14.7 0.2 fusion.30
  15.0 0.1 reshape.63
  15.1 1.5 fusion.26
  16.6 2.4 fusion.22
  19.0 0.2 fusion.32
  19.2 0.1 reshape.66
  19.3 0.1 reshape.68
  19.4 20.3 %all-gather = f32[16,1,12288]{2,1,0:T(1,128)S(1)} all-gather(f32[1,1,12288]{2,1,0:T(1,128)S(1)} %reshape.68), channel_id=1, replica_groups=mesh['train'=16,'query'=16] {'query'}, dimensions={0}, use_global_device_ids=true | all-gather | bytes 835584 | tf_op jit(solution)/shard_map/all_gather | solution.py:70
  39.7 1.4 copy.17
  41.1 82.2 %all-gather.3.cloned.1.call-done = f32[256,12288]{1,0:T(8,128)} async-done(((f32[16,12288]{1,0:T(8,128)}), f32[256,12288]{1,0:T(8,128)}) %all-gather.3.cloned.1.call-update) | async-done | bytes 12582928 | tf_op jit(solution)/shard_map/all_gather | solution.py:71
  123.3 11.5 %fusion.10 = f32[256,256]{0,1:T(8,128)S(1)} fusion(f32[256,12288]{1,0:T(8,128)} %all-gather.3.cloned.1.call-done), kind=kOutput, calls=%fused_computation.13 | convolution fusion | flops 3221225472 | bytes 8650752 | tf_op jit(solution)/shard_map/dot_general | solution.py:77
  134.9 11.6 %fusion.12 = f32[256,256]{0,1:T(8,128)S(1)} fusion(f32[256,12288]{1,0:T(8,128)} %all-gather.3.cloned.1.call-done), kind=kOutput, calls=%fused_computation.15 | convolution fusion | flops 3221225472 | bytes 8650752 | tf_op jit(solution)/shard_map/dot_general | solution.py:77
  146.5 3.5 %fusion.17 = f32[256,256]{0,1:T(8,128)S(1)} fusion(f32[256,12288]{1,0:T(8,128)S(1)} %copy-done.1), kind=kOutput, calls=%fused_computation.20 | convolution fusion | flops 3221225472 | bytes 4456448 | tf_op jit(solution)/shard_map/dot_general | solution.py:77
  150.0 3.5 %fusion.8 = f32[256,256]{0,1:T(8,128)S(1)} fusion(f32[256,12288]{1,0:T(8,128)S(1)} %copy-done.1), kind=kOutput, calls=%fused_computation.11 | convolution fusion | flops 3221225472 | bytes 4456448 | tf_op jit(solution)/shard_map/dot_general | solution.py:77
  153.6 0.7 copy-done.4
  154.3 0.8 select_reduce_fusion.1
  155.7 1.1 select_add_fusion
  156.8 11.8 %fusion.3 = f32[256,256]{1,0:T(8,128)S(1)} fusion(f32[256,12288]{1,0:T(8,128)} %all-gather.3.cloned.1.call-done), kind=kOutput, calls=%fused_computation.6 | convolution fusion | flops 3221225472 | bytes 8650752 | tf_op jit(solution)/shard_map/dot_general | solution.py:85
  168.6 11.7 %fusion.5 = f32[256,256]{1,0:T(8,128)S(1)} fusion(f32[256,12288]{1,0:T(8,128)} %all-gather.3.cloned.1.call-done), kind=kOutput, calls=%fused_computation.8 | convolution fusion | flops 3221225472 | bytes 8650752 | tf_op jit(solution)/shard_map/dot_general | solution.py:85
  180.4 2.6 copy.12
  183.0 1.4 multiply_reduce_fusion.1
  184.4 0.7 reduce_max.9
  185.0 0.7 multiply_divide_fusion
  185.7 1.2 fusion.25
  187.0 86.5 %while.13 = (s32[]{:T(128)}, f32[512,512]{0,1:T(8,128)}, f32[]{:T(128)}, f32[512,512]{1,0:T(8,128)}, s32[]{:T(128)}) while((s32[]{:T(128)}, f32[512,512]{0,1:T(8,128)}, f32[]{:T(128)}, f32[512,512]{1,0:T(8,128)}, s32[]{:T(128)}) %tuple.29), condition=%wide.region_6.0_spmd.clone, body=%wide.region_4.0_spmd.clone.sunk | while | flops 3222798336 | bytes 8388693 | solution.py:46
  187.0 1.2 copy.31
  188.2 3.8 %multiply_reduce_fusion.3 = (f32[]{:T(128)}, f32[512,512]{1,0:T(8,128)S(1)}) fusion(f32[512,512]{1,0:T(8,128)} %get-tuple-element.108, f32[512,512]{0,1:T(8,128)S(1)} %copy.31), kind=kOutput, calls=%fused_computation.5.clone.1 | convolution fusion | flops 1611923456 | bytes 3145732 | tf_op jit(solution)/shard_map/while/body/dot_general | solution.py:42
  192.0 2.9 fusion.61
  195.6 1.2 copy.31
  196.8 3.8 %multiply_reduce_fusion.3 = (f32[]{:T(128)}, f32[512,512]{1,0:T(8,128)S(1)}) fusion(f32[512,512]{1,0:T(8,128)} %get-tuple-element.108, f32[512,512]{0,1:T(8,128)S(1)} %copy.31), kind=kOutput, calls=%fused_computation.5.clone.1 | convolution fusion | flops 1611923456 | bytes 3145732 | tf_op jit(solution)/shard_map/while/body/dot_general | solution.py:42
  200.6 2.9 fusion.61
  204.2 1.2 copy.31
  205.4 3.8 %multiply_reduce_fusion.3 = (f32[]{:T(128)}, f32[512,512]{1,0:T(8,128)S(1)}) fusion(f32[512,512]{1,0:T(8,128)} %get-tuple-element.108, f32[512,512]{0,1:T(8,128)S(1)} %copy.31), kind=kOutput, calls=%fused_computation.5.clone.1 | convolution fusion | flops 1611923456 | bytes 3145732 | tf_op jit(solution)/shard_map/while/body/dot_general | solution.py:42
  209.3 2.9 %fusion.61 = f32[512,512]{0,1:T(8,128)} fusion(f32[512,512]{0,1:T(8,128)S(1)} %copy.31, f32[512,512]{1,0:T(8,128)S(1)} %get-tuple-element.93), kind=kOutput, calls=%fused_computation.2.clone.1 | convolution fusion | flops 1610874880 | bytes 3145728 | tf_op jit(solution)/shard_map/while/body/dot_general | solution.py:44
  212.8 1.2 copy.31
  214.1 3.8 %multiply_reduce_fusion.3 = (f32[]{:T(128)}, f32[512,512]{1,0:T(8,128)S(1)}) fusion(f32[512,512]{1,0:T(8,128)} %get-tuple-element.108, f32[512,512]{0,1:T(8,128)S(1)} %copy.31), kind=kOutput, calls=%fused_computation.5.clone.1 | convolution fusion | flops 1611923456 | bytes 3145732 | tf_op jit(solution)/shard_map/while/body/dot_general | solution.py:42
  217.9 2.9 fusion.61
  221.4 1.2 copy.31
  222.7 3.8 %multiply_reduce_fusion.3 = (f32[]{:T(128)}, f32[512,512]{1,0:T(8,128)S(1)}) fusion(f32[512,512]{1,0:T(8,128)} %get-tuple-element.108, f32[512,512]{0,1:T(8,128)S(1)} %copy.31), kind=kOutput, calls=%fused_computation.5.clone.1 | convolution fusion | flops 1611923456 | bytes 3145732 | tf_op jit(solution)/shard_map/while/body/dot_general | solution.py:42
  226.5 2.9 fusion.61
  230.1 1.2 copy.31
  231.3 3.8 %multiply_reduce_fusion.3 = (f32[]{:T(128)}, f32[512,512]{1,0:T(8,128)S(1)}) fusion(f32[512,512]{1,0:T(8,128)} %get-tuple-element.108, f32[512,512]{0,1:T(8,128)S(1)} %copy.31), kind=kOutput, calls=%fused_computation.5.clone.1 | convolution fusion | flops 1611923456 | bytes 3145732 | tf_op jit(solution)/shard_map/while/body/dot_general | solution.py:42
  235.1 2.9 %fusion.61 = f32[512,512]{0,1:T(8,128)} fusion(f32[512,512]{0,1:T(8,128)S(1)} %copy.31, f32[512,512]{1,0:T(8,128)S(1)} %get-tuple-element.93), kind=kOutput, calls=%fused_computation.2.clone.1 | convolution fusion | flops 1610874880 | bytes 3145728 | tf_op jit(solution)/shard_map/while/body/dot_general | solution.py:44
  238.7 1.2 copy.31
  239.9 3.8 %multiply_reduce_fusion.3 = (f32[]{:T(128)}, f32[512,512]{1,0:T(8,128)S(1)}) fusion(f32[512,512]{1,0:T(8,128)} %get-tuple-element.108, f32[512,512]{0,1:T(8,128)S(1)} %copy.31), kind=kOutput, calls=%fused_computation.5.clone.1 | convolution fusion | flops 1611923456 | bytes 3145732 | tf_op jit(solution)/shard_map/while/body/dot_general | solution.py:42
  243.8 2.9 fusion.61
  247.3 1.2 copy.31
  248.5 3.8 %multiply_reduce_fusion.3 = (f32[]{:T(128)}, f32[512,512]{1,0:T(8,128)S(1)}) fusion(f32[512,512]{1,0:T(8,128)} %get-tuple-element.108, f32[512,512]{0,1:T(8,128)S(1)} %copy.31), kind=kOutput, calls=%fused_computation.5.clone.1 | convolution fusion | flops 1611923456 | bytes 3145732 | tf_op jit(solution)/shard_map/while/body/dot_general | solution.py:42
  252.4 2.9 fusion.61
  255.9 1.2 copy.31
  257.2 3.8 %multiply_reduce_fusion.3 = (f32[]{:T(128)}, f32[512,512]{1,0:T(8,128)S(1)}) fusion(f32[512,512]{1,0:T(8,128)} %get-tuple-element.108, f32[512,512]{0,1:T(8,128)S(1)} %copy.31), kind=kOutput, calls=%fused_computation.5.clone.1 | convolution fusion | flops 1611923456 | bytes 3145732 | tf_op jit(solution)/shard_map/while/body/dot_general | solution.py:42
  261.0 2.9 %fusion.61 = f32[512,512]{0,1:T(8,128)} fusion(f32[512,512]{0,1:T(8,128)S(1)} %copy.31, f32[512,512]{1,0:T(8,128)S(1)} %get-tuple-element.93), kind=kOutput, calls=%fused_computation.2.clone.1 | convolution fusion | flops 1610874880 | bytes 3145728 | tf_op jit(solution)/shard_map/while/body/dot_general | solution.py:44
  264.6 1.2 copy.31
  265.8 3.8 %multiply_reduce_fusion.3 = (f32[]{:T(128)}, f32[512,512]{1,0:T(8,128)S(1)}) fusion(f32[512,512]{1,0:T(8,128)} %get-tuple-element.108, f32[512,512]{0,1:T(8,128)S(1)} %copy.31), kind=kOutput, calls=%fused_computation.5.clone.1 | convolution fusion | flops 1611923456 | bytes 3145732 | tf_op jit(solution)/shard_map/while/body/dot_general | solution.py:42
  269.6 2.9 fusion.61
  273.5 3.1 %fusion.33 = f32[512,256]{1,0:T(8,128)S(1)} fusion(f32[512,512]{0,1:T(8,128)} %get-tuple-element.35, f32[512,256]{1,0:T(8,128)S(1)} %pad_maximum_fusion), kind=kOutput, calls=%fused_computation.51 | convolution fusion | flops 805306368 | bytes 2097152 | tf_op jit(solution)/shard_map/dot_general | solution.py:49
  276.6 3.0 %convolution_subtract_fusion.1 = f32[512,256]{1,0:T(8,128)S(1)} fusion(f32[512,256]{1,0:T(8,128)S(1)} %pad_maximum_fusion, f32[512,512]{0,1:T(8,128)} %copy-done.3, f32[512,256]{1,0:T(8,128)S(1)} %fusion.33), kind=kOutput, calls=%fused_computation.25 | convolution fusion | flops 805437440 | bytes 2621440 | tf_op jit(solution)/shard_map/dot_general | solution.py:51
  279.6 1.8 fusion.21
  281.5 0.6 pad_maximum_fusion.2
  (21 shorter events, 0.2 us)
Async XLA Ops:
  6.5 10.1 %copy-start = (bf16[1,96,14336]{2,1,0:T(8,128)(2,1)S(1)}, bf16[1,96,14336]{2,1,0:T(8,128)(2,1)}, u32[]{:S(2)}) copy-start(bf16[1,96,14336]{2,1,0:T(8,128)(2,1)} %param.14) | copy-start | bytes 8257540
  6.5 116.8 %all-gather.3.cloned.1.call-start = ((), (), s32[]{:S(2)}) async-start(), calls=%async_computation | async-start | bytes 13369344 | tf_op jit(solution)/shard_map/all_gather | solution.py:71
  7.5 5.2 %copy-start.5 = (bf16[4096,64]{0,1:T(8,128)(2,1)S(1)}, bf16[4096,64]{0,1:T(8,128)(2,1)}, u32[]{:S(2)}) copy-start(bf16[4096,64]{0,1:T(8,128)(2,1)} %param.16) | copy-start | bytes 1572868
  7.5 7.6 %copy-start.6 = (s32[1,96]{1,0:T(1,128)S(1)}, s32[1,96]{1,0:T(1,128)}, u32[]{:S(2)}) copy-start(s32[1,96]{1,0:T(1,128)} %param.15) | copy-start | bytes 1156
  123.3 23.1 %copy-start.1 = (f32[256,12288]{1,0:T(8,128)S(1)}, f32[256,12288]{1,0:T(8,128)}, u32[]{:S(2)}) copy-start(f32[256,12288]{1,0:T(8,128)} %all-gather.3.cloned.1.call-done) | copy-start | bytes 37748740
  153.6 0.7 copy-start.4
  156.8 23.5 %copy-start.3 = (f32[512,512]{0,1:T(8,128)}, f32[512,512]{0,1:T(8,128)S(1)}, u32[]{:S(2)}) copy-start(f32[512,512]{0,1:T(8,128)S(1)} %select_add_fusion) | copy-start | bytes 3145732
  273.4 6.2 %copy-start.2 = (f32[512,512]{0,1:T(8,128)S(1)}, f32[512,512]{0,1:T(8,128)}, u32[]{:S(2)}) copy-start(f32[512,512]{0,1:T(8,128)} %get-tuple-element.35) | copy-start | bytes 3145732
Sparse Core Ops, SparseCore 0:
  41.2 82.0 all-gather.2
